TPU v7x, 32 devices: a whole 2x2x4 slice. The times are simulated.
32 devices in a mesh: rows: 8 (over z, x), samp: 4 (over y, core).
Axes of the slice: x: 2, y: 2, z: 4, core: 2. Of those that a mesh axis runs over, the one named last changes fastest.
Arguments:
- noise: bfloat16 [6, 64, 512, 128], P(None, 'rows', 'samp'), may hold values from -6 to 6
- diag_inverse: bfloat16 [6, 64, 128, 128], P(None, 'rows'), may hold values from -0.5 to 0.5
- coupling: bfloat16 [5, 64, 16, 128, 128], P(None, 'rows'), may hold values from -0.125 to 0.125
- pattern: int32 [5, 64, 16], P(None, 'rows'), may hold values from 0 to 319, as said below
Outputs:
- samples: bfloat16 [6, 64, 512, 128], P(None, 'rows', 'samp')
- variance: float32 [6, 64, 128], P(None, 'rows')
Inputs may be any that keep to these rules, and one draw needn't show every extreme that they name: pattern[l, s, k] names a block row of a level before l + 1; the entry k = 0 lies in level l; entries may repeat. Block rows s with equal s // 8 together name, within any one level, at most one of the block rows t that share one value of t // 8.
All inputs are finite; a program needn't handle non-finite values.
Results may differ from a plain program's by a relative error of at most 0.008.
Values may be sent and summed in bfloat16 or wider, within the bound.
A program may use at most 192 MiB of HBM per device.

v0:
```python
import jax
import jax.numpy as jnp
from jax import lax
from jax.sharding import PartitionSpec as P


def solve_block(residual, inverse):
    rounded = residual.astype(jnp.bfloat16)
    return jnp.einsum("psb,pbc->psc", rounded, inverse, preferred_element_type=jnp.float32).astype(
        jnp.bfloat16
    )


def contribution(picked, blocks):
    return jnp.einsum("pksb,pkbc->psc", picked, blocks, preferred_element_type=jnp.float32)


def body(noise, diag_inverse, coupling, pattern):
    levels = noise.shape[0]
    slot_dev = noise.shape[1]
    device_count = lax.axis_size("rows")
    slot_total = slot_dev * device_count
    owned = [solve_block(noise[0], diag_inverse[0])]
    table = lax.all_gather(pattern, "rows", axis=1, tiled=True)
    entries = table.reshape(levels - 1, device_count, slot_dev * table.shape[2])
    entries = jnp.transpose(entries, (1, 0, 2)).reshape(device_count, -1)
    my_index = lax.axis_index("rows")
    pending = [None] + [noise[target].astype(jnp.float32) for target in range(1, levels)]
    for source in range(levels - 1):
        if source > 0:
            owned.append(solve_block(pending[source], diag_inverse[source]))
        block = owned[source]
        base = source * slot_total + my_index * slot_dev
        hit = jnp.logical_and(entries >= base, entries < base + slot_dev)
        wanted = jnp.max(jnp.where(hit, entries - base, 0), axis=1)
        outgoing = jnp.take(block, wanted, axis=0)
        incoming = lax.all_to_all(outgoing, "rows", split_axis=0, concat_axis=0, tiled=True)
        for target in range(source + 1, levels):
            refs = pattern[target - 1] - source * slot_total
            inside = jnp.logical_and(refs >= 0, refs < slot_total)
            holder = jnp.clip(refs // slot_dev, 0, device_count - 1)
            picked = jnp.take(incoming, holder, axis=0)
            picked = picked * inside.astype(jnp.bfloat16)[:, :, None, None]
            pending[target] = pending[target] - contribution(picked, coupling[target - 1])
    owned.append(solve_block(pending[levels - 1], diag_inverse[levels - 1]))
    samples = jnp.stack(owned, axis=0)
    wide = samples.astype(jnp.float32)
    local_sums = jnp.sum(wide * wide, axis=2)
    totals = lax.psum(local_sums, "samp")
    variance = totals / (samples.shape[2] * lax.axis_size("samp"))
    return (samples, variance)


def solution(mesh):
    placed = (
        P(None, "rows", "samp", None),
        P(None, "rows", None, None),
        P(None, "rows", None, None, None),
        P(None, "rows", None),
    )
    return jax.shard_map(
        body,
        mesh=mesh,
        in_specs=placed,
        out_specs=(P(None, "rows", "samp", None), P(None, "rows", None)),
        check_vma=False,
    )
```

profile of v0, /device:TPU:0, one launch (start us, length us, event | category | flops | bytes accessed | tf_op | source)
XLA Modules:
  0.0 212.7 jit_solution(17466377235960247067)
XLA Ops:
  0.6 32.6 %all_gather.3 = s32[5,64,16]{2,1,0:T(8,128)S(1)} all-gather(s32[5,8,16]{2,1,0:T(8,128)} %param.11), channel_id=1, replica_groups=mesh['rows'=8,'samp'=4] {'rows'}, dimensions={1}, use_global_device_ids=true | all-gather | bytes 23040 | tf_op jit(solution)/shard_map/all_gather | solution.py:24
  36.4 5.5 %all-to-all-start = ((bf16[8,128,128]{2,1,0:T(8,128)(2,1)}), bf16[8,128,128]{2,1,0:T(8,128)(2,1)S(1)}, u32[]{:S(2)}, u32[]{:S(2)}) async-start(bf16[8,128,128]{2,1,0:T(8,128)(2,1)} %broadcast_select_fusion.4), calls=%async_computation | async-start | bytes 524288 | tf_op jit(solution)/shard_map/all_to_all | solution.py:37
  45.7 4.4 %all-to-all-done = bf16[8,128,128]{2,1,0:T(8,128)(2,1)S(1)} async-done(((bf16[8,128,128]{2,1,0:T(8,128)(2,1)}), bf16[8,128,128]{2,1,0:T(8,128)(2,1)S(1)}, u32[]{:S(2)}, u32[]{:S(2)}) %all-to-all-start) | async-done | bytes 262176 | tf_op jit(solution)/shard_map/all_to_all | solution.py:37
  53.1 5.0 %bitcast_dynamic-update-slice_fusion.3 = (bf16[6,8,128,128]{3,2,1,0:T(8,128)(2,1)S(1)}, bf16[8,128,128]{2,1,0:T(8,128)(2,1)S(1)}) fusion(bf16[6,8,128,128]{3,2,1,0:T(8,128)(2,1)S(1)} %get-tuple-element.81, bf16[6,8,128,128]{3,2,1,0:T(8,128)(2,1)} %param.9, bf16[5,8,16,128,128]{4,3,2,1,0:T(8,128)(2,1)} %param.10, bf16[8,16,128,128]{3,2,1,0:T(8,128)(2,1)} %bitcast.497, ...), kind=kOutput, calls=%fused_computation.178 | convolution fusion | flops 575143936 | bytes 9440256 | tf_op jit(solution)/shard_map/psb,pbc->psc/dot_general | solution.py:9
  59.6 3.6 %all-to-all-start.1 = ((bf16[8,128,128]{2,1,0:T(8,128)(2,1)}), bf16[8,128,128]{2,1,0:T(8,128)(2,1)S(1)}, u32[]{:S(2)}, u32[]{:S(2)}) async-start(bf16[8,128,128]{2,1,0:T(8,128)(2,1)} %broadcast_select_fusion.3), calls=%async_computation.1 | async-start | bytes 524288 | tf_op jit(solution)/shard_map/all_to_all | solution.py:37
  63.2 3.0 %gather_fusion.2 = bf16[128,128,128]{2,1,0:T(8,128)(2,1)} fusion(bf16[8,128,128]{2,1,0:T(8,128)(2,1)S(1)} %all-to-all-done, s32[1024]{0:T(1024)S(1)} %get-tuple-element.106), kind=kCustom, calls=%fused_computation.6.clone | custom fusion | bytes 8389120 | tf_op jit(solution)/shard_map/jit(_take)/gather | solution.py:42
  66.2 4.9 %fusion.174 = f32[8,128,128]{2,1,0:T(8,128)S(1)} fusion(bf16[5,8,16,128,128]{4,3,2,1,0:T(8,128)(2,1)} %param.10, bf16[8,16,128,128]{3,2,1,0:T(8,128)(2,1)} %bitcast.505, pred[8,16]{1,0:T(8,128)(4,1)S(1)} %get-tuple-element.75, bf16[8,16]{1,0:T(8,128)(2,1)S(1)} %get-tuple-element.70, bf16[6,8,128,128]{3,2,1,0:T(8,128)(2,1)} %param.8), kind=kOutput, calls=%fused_computation.154 | convolution fusion | flops 541327360 | bytes 9175424 | tf_op jit(solution)/shard_map/pksb,pkbc->psc/dot_general | solution.py:15
  74.1 5.7 %fusion.168 = f32[8,128,128]{2,1,0:T(8,128)} fusion(bf16[5,8,16,128,128]{4,3,2,1,0:T(8,128)(2,1)} %param.10, bf16[8,16,128,128]{3,2,1,0:T(8,128)(2,1)} %bitcast.506, pred[8,16]{1,0:T(8,128)(4,1)S(1)} %get-tuple-element.73, bf16[8,16]{1,0:T(8,128)(2,1)S(1)} %get-tuple-element.65, bf16[6,8,128,128]{3,2,1,0:T(8,128)(2,1)} %param.8), kind=kOutput, calls=%fused_computation.152 | convolution fusion | flops 541327360 | bytes 9175424 | tf_op jit(solution)/shard_map/pksb,pkbc->psc/dot_general | solution.py:15
  82.7 5.7 %fusion.159 = f32[8,128,128]{2,1,0:T(8,128)} fusion(bf16[5,8,16,128,128]{4,3,2,1,0:T(8,128)(2,1)} %param.10, bf16[8,16,128,128]{3,2,1,0:T(8,128)(2,1)} %bitcast.507, pred[8,16]{1,0:T(8,128)(4,1)S(1)} %get-tuple-element.79, bf16[8,16]{1,0:T(8,128)(2,1)S(1)} %get-tuple-element.57, bf16[6,8,128,128]{3,2,1,0:T(8,128)(2,1)} %param.8), kind=kOutput, calls=%fused_computation.149 | convolution fusion | flops 541327360 | bytes 9175424 | tf_op jit(solution)/shard_map/pksb,pkbc->psc/dot_general | solution.py:15
  91.4 5.7 %fusion.147 = f32[8,128,128]{2,1,0:T(8,128)} fusion(bf16[5,8,16,128,128]{4,3,2,1,0:T(8,128)(2,1)} %param.10, bf16[8,16,128,128]{3,2,1,0:T(8,128)(2,1)} %bitcast.501, pred[8,16]{1,0:T(8,128)(4,1)S(1)} %get-tuple-element.17, bf16[8,16]{1,0:T(8,128)(2,1)S(1)} %get-tuple-element.47, bf16[6,8,128,128]{3,2,1,0:T(8,128)(2,1)} %param.8), kind=kOutput, calls=%fused_computation.145 | convolution fusion | flops 541327360 | bytes 9175424 | tf_op jit(solution)/shard_map/pksb,pkbc->psc/dot_general | solution.py:15
  100.1 5.0 %bitcast_dynamic-update-slice_fusion.2 = (bf16[6,8,128,128]{3,2,1,0:T(8,128)(2,1)S(1)}, bf16[8,128,128]{2,1,0:T(8,128)(2,1)S(1)}) fusion(bf16[6,8,128,128]{3,2,1,0:T(8,128)(2,1)S(1)} %get-tuple-element.83, bf16[6,8,128,128]{3,2,1,0:T(8,128)(2,1)} %param.9, f32[8,128,128]{2,1,0:T(8,128)S(1)} %fusion.174, bf16[5,8,16,128,128]{4,3,2,1,0:T(8,128)(2,1)} %param.10, ...), kind=kOutput, calls=%fused_computation.176 | convolution fusion | flops 575012864 | bytes 9702400 | tf_op jit(solution)/shard_map/psb,pbc->psc/dot_general | solution.py:9
  106.6 5.8 %all-to-all-start.2 = ((bf16[8,128,128]{2,1,0:T(8,128)(2,1)}), bf16[8,128,128]{2,1,0:T(8,128)(2,1)S(1)}, u32[]{:S(2)}, u32[]{:S(2)}) async-start(bf16[8,128,128]{2,1,0:T(8,128)(2,1)} %broadcast_select_fusion.2), calls=%async_computation.2 | async-start | bytes 524288 | tf_op jit(solution)/shard_map/all_to_all | solution.py:37
  115.3 4.9 %fusion.165 = f32[8,128,128]{2,1,0:T(8,128)S(1)} fusion(f32[8,128,128]{2,1,0:T(8,128)} %fusion.168, bf16[5,8,16,128,128]{4,3,2,1,0:T(8,128)(2,1)} %param.10, bf16[8,16,128,128]{3,2,1,0:T(8,128)(2,1)} %bitcast.502, pred[8,16]{1,0:T(8,128)(4,1)S(1)} %get-tuple-element.61, bf16[8,16]{1,0:T(8,128)(2,1)S(1)} %get-tuple-element.67), kind=kOutput, calls=%fused_computation.151 | convolution fusion | flops 541196288 | bytes 9437568 | tf_op jit(solution)/shard_map/pksb,pkbc->psc/dot_general | solution.py:15
  123.3 5.7 %fusion.156 = f32[8,128,128]{2,1,0:T(8,128)} fusion(f32[8,128,128]{2,1,0:T(8,128)} %fusion.159, bf16[5,8,16,128,128]{4,3,2,1,0:T(8,128)(2,1)} %param.10, bf16[8,16,128,128]{3,2,1,0:T(8,128)(2,1)} %bitcast.503, pred[8,16]{1,0:T(8,128)(4,1)S(1)} %get-tuple-element.53, bf16[8,16]{1,0:T(8,128)(2,1)S(1)} %get-tuple-element.59), kind=kOutput, calls=%fused_computation.148 | convolution fusion | flops 541196288 | bytes 9437568 | tf_op jit(solution)/shard_map/pksb,pkbc->psc/dot_general | solution.py:15
  132.0 5.7 %fusion.144 = f32[8,128,128]{2,1,0:T(8,128)} fusion(f32[8,128,128]{2,1,0:T(8,128)} %fusion.147, bf16[5,8,16,128,128]{4,3,2,1,0:T(8,128)(2,1)} %param.10, bf16[8,16,128,128]{3,2,1,0:T(8,128)(2,1)} %bitcast.498, pred[8,16]{1,0:T(8,128)(4,1)S(1)} %get-tuple-element.45, bf16[8,16]{1,0:T(8,128)(2,1)S(1)} %get-tuple-element.48), kind=kOutput, calls=%fused_computation.144 | convolution fusion | flops 541196288 | bytes 9437568 | tf_op jit(solution)/shard_map/pksb,pkbc->psc/dot_general | solution.py:15
  140.7 5.0 %bitcast_dynamic-update-slice_fusion.1 = (bf16[6,8,128,128]{3,2,1,0:T(8,128)(2,1)S(1)}, bf16[8,128,128]{2,1,0:T(8,128)(2,1)S(1)}) fusion(bf16[6,8,128,128]{3,2,1,0:T(8,128)(2,1)S(1)} %get-tuple-element.85, bf16[6,8,128,128]{3,2,1,0:T(8,128)(2,1)} %param.9, f32[8,128,128]{2,1,0:T(8,128)S(1)} %fusion.165, bf16[5,8,16,128,128]{4,3,2,1,0:T(8,128)(2,1)} %param.10, ...), kind=kOutput, calls=%fused_computation.174 | convolution fusion | flops 575012864 | bytes 9702400 | tf_op jit(solution)/shard_map/psb,pbc->psc/dot_general | solution.py:9
  147.2 6.0 %all-to-all-start.3 = ((bf16[8,128,128]{2,1,0:T(8,128)(2,1)}), bf16[8,128,128]{2,1,0:T(8,128)(2,1)S(1)}, u32[]{:S(2)}, u32[]{:S(2)}) async-start(bf16[8,128,128]{2,1,0:T(8,128)(2,1)} %broadcast_select_fusion.1), calls=%async_computation.3 | async-start | bytes 524288 | tf_op jit(solution)/shard_map/all_to_all | solution.py:37
  156.2 4.9 %fusion.153 = f32[8,128,128]{2,1,0:T(8,128)S(1)} fusion(f32[8,128,128]{2,1,0:T(8,128)} %fusion.156, bf16[5,8,16,128,128]{4,3,2,1,0:T(8,128)(2,1)} %param.10, bf16[8,16,128,128]{3,2,1,0:T(8,128)(2,1)} %bitcast.504, pred[8,16]{1,0:T(8,128)(4,1)S(1)} %get-tuple-element.51, bf16[8,16]{1,0:T(8,128)(2,1)S(1)} %get-tuple-element.60), kind=kOutput, calls=%fused_computation.147 | convolution fusion | flops 541196288 | bytes 9437568 | tf_op jit(solution)/shard_map/pksb,pkbc->psc/dot_general | solution.py:15
  164.1 5.7 %fusion.141 = f32[8,128,128]{2,1,0:T(8,128)} fusion(f32[8,128,128]{2,1,0:T(8,128)} %fusion.144, bf16[5,8,16,128,128]{4,3,2,1,0:T(8,128)(2,1)} %param.10, bf16[8,16,128,128]{3,2,1,0:T(8,128)(2,1)} %bitcast.499, pred[8,16]{1,0:T(8,128)(4,1)S(1)} %get-tuple-element.43, bf16[8,16]{1,0:T(8,128)(2,1)S(1)} %get-tuple-element.49), kind=kOutput, calls=%fused_computation.143 | convolution fusion | flops 541196288 | bytes 9437568 | tf_op jit(solution)/shard_map/pksb,pkbc->psc/dot_general | solution.py:15
  172.8 5.0 %bitcast_dynamic-update-slice_fusion = (bf16[6,8,128,128]{3,2,1,0:T(8,128)(2,1)S(1)}, bf16[8,128,128]{2,1,0:T(8,128)(2,1)S(1)}) fusion(bf16[6,8,128,128]{3,2,1,0:T(8,128)(2,1)S(1)} %get-tuple-element.87, bf16[6,8,128,128]{3,2,1,0:T(8,128)(2,1)} %param.9, f32[8,128,128]{2,1,0:T(8,128)S(1)} %fusion.153, bf16[5,8,16,128,128]{4,3,2,1,0:T(8,128)(2,1)} %param.10, ...), kind=kOutput, calls=%fused_computation.172 | convolution fusion | flops 575012864 | bytes 9702400 | tf_op jit(solution)/shard_map/psb,pbc->psc/dot_general | solution.py:9
  179.2 6.0 %all-to-all-start.4 = ((bf16[8,128,128]{2,1,0:T(8,128)(2,1)}), bf16[8,128,128]{2,1,0:T(8,128)(2,1)S(1)}, u32[]{:S(2)}, u32[]{:S(2)}) async-start(bf16[8,128,128]{2,1,0:T(8,128)(2,1)} %broadcast_select_fusion), calls=%async_computation.4 | async-start | bytes 524288 | tf_op jit(solution)/shard_map/all_to_all | solution.py:37
  188.3 4.9 %fusion.138 = f32[8,128,128]{2,1,0:T(8,128)S(1)} fusion(f32[8,128,128]{2,1,0:T(8,128)S(1)} %copy-done.1, bf16[5,8,16,128,128]{4,3,2,1,0:T(8,128)(2,1)} %param.10, bf16[8,16,128,128]{3,2,1,0:T(8,128)(2,1)} %bitcast.500, pred[8,16]{1,0:T(8,128)(4,1)S(1)} %get-tuple-element.41, bf16[8,16]{1,0:T(8,128)(2,1)S(1)} %get-tuple-element.50), kind=kOutput, calls=%fused_computation.142 | convolution fusion | flops 541196288 | bytes 9437568 | tf_op jit(solution)/shard_map/pksb,pkbc->psc/dot_general | solution.py:15
  196.5 5.0 %fusion.196 = bf16[6,8,128,128]{3,2,1,0:T(8,128)(2,1)S(1)} fusion(bf16[6,8,128,128]{3,2,1,0:T(8,128)(2,1)S(1)} %get-tuple-element.89, f32[8,128,128]{2,1,0:T(8,128)S(1)} %fusion.138, bf16[5,8,16,128,128]{4,3,2,1,0:T(8,128)(2,1)} %param.10, bf16[8,16,128,128]{3,2,1,0:T(8,128)(2,1)} %bitcast.496, pred[8,16]{1,0:T(8,128)(4,1)S(1)} %get-tuple-element.9, ...), kind=kOutput, calls=%fused_computation.168 | convolution fusion | flops 575012864 | bytes 9440256 | tf_op jit(solution)/shard_map/psb,pbc->psc/dot_general | solution.py:9
  201.9 10.3 %psum.7 = f32[6,8,128]{2,1,0:T(8,128)S(1)} all-reduce(f32[6,8,128]{2,1,0:T(8,128)S(1)} %multiply_reduce_fusion), channel_id=1, replica_groups=mesh['rows'=8,'samp'=4] {'samp'}, use_global_device_ids=true, to_apply=%region_11.14 | all-reduce | flops 6144 | bytes 49152 | tf_op jit(solution)/shard_map/psum | solution.py:49
  (85 shorter events, 55.8 us)
Async XLA Ops:
  36.4 13.7 %all-to-all-start = ((bf16[8,128,128]{2,1,0:T(8,128)(2,1)}), bf16[8,128,128]{2,1,0:T(8,128)(2,1)S(1)}, u32[]{:S(2)}, u32[]{:S(2)}) async-start(bf16[8,128,128]{2,1,0:T(8,128)(2,1)} %broadcast_select_fusion.4), calls=%async_computation | async-start | bytes 524288 | tf_op jit(solution)/shard_map/all_to_all | solution.py:37
  59.6 37.5 %all-to-all-start.1 = ((bf16[8,128,128]{2,1,0:T(8,128)(2,1)}), bf16[8,128,128]{2,1,0:T(8,128)(2,1)S(1)}, u32[]{:S(2)}, u32[]{:S(2)}) async-start(bf16[8,128,128]{2,1,0:T(8,128)(2,1)} %broadcast_select_fusion.3), calls=%async_computation.1 | async-start | bytes 524288 | tf_op jit(solution)/shard_map/all_to_all | solution.py:37
  106.6 31.2 %all-to-all-start.2 = ((bf16[8,128,128]{2,1,0:T(8,128)(2,1)}), bf16[8,128,128]{2,1,0:T(8,128)(2,1)S(1)}, u32[]{:S(2)}, u32[]{:S(2)}) async-start(bf16[8,128,128]{2,1,0:T(8,128)(2,1)} %broadcast_select_fusion.2), calls=%async_computation.2 | async-start | bytes 524288 | tf_op jit(solution)/shard_map/all_to_all | solution.py:37
  147.2 22.7 %all-to-all-start.3 = ((bf16[8,128,128]{2,1,0:T(8,128)(2,1)}), bf16[8,128,128]{2,1,0:T(8,128)(2,1)S(1)}, u32[]{:S(2)}, u32[]{:S(2)}) async-start(bf16[8,128,128]{2,1,0:T(8,128)(2,1)} %broadcast_select_fusion.1), calls=%async_computation.3 | async-start | bytes 524288 | tf_op jit(solution)/shard_map/all_to_all | solution.py:37
  179.2 14.2 %all-to-all-start.4 = ((bf16[8,128,128]{2,1,0:T(8,128)(2,1)}), bf16[8,128,128]{2,1,0:T(8,128)(2,1)S(1)}, u32[]{:S(2)}, u32[]{:S(2)}) async-start(bf16[8,128,128]{2,1,0:T(8,128)(2,1)} %broadcast_select_fusion), calls=%async_computation.4 | async-start | bytes 524288 | tf_op jit(solution)/shard_map/all_to_all | solution.py:37
  185.2 3.0 %copy-start.1 = (f32[8,128,128]{2,1,0:T(8,128)S(1)}, f32[8,128,128]{2,1,0:T(8,128)}, u32[]{:S(2)}) copy-start(f32[8,128,128]{2,1,0:T(8,128)} %fusion.141) | copy-start | bytes 1572868
  201.5 11.3 %copy-start = (bf16[6,8,128,128]{3,2,1,0:T(8,128)(2,1)}, bf16[6,8,128,128]{3,2,1,0:T(8,128)(2,1)S(1)}, u32[]{:S(2)}) copy-start(bf16[6,8,128,128]{3,2,1,0:T(8,128)(2,1)S(1)} %fusion.196) | copy-start | bytes 4718596
where the time goes:
time: 214 us; the launch traced here: 213 us
  matrix products  80.1 us (37%)
  local copies, waits for them, and re-layouts  49.7 us (23%)
  blocking collectives  42.8 us (20%)
  starting transfers between devices  26.8 us (13%)
  other arithmetic  7.59 us (4%)
  waiting for transfers between devices  4.68 us (2%)
    dot_general x10, matrix products, contribution(): jnp.einsum('pksb,pkbc->psc', picked, blocks, preferred_element_type=jnp.f...  53.8 us
    gather x15, local copies, waits for them, and re-layouts, body(): picked = jnp.take(incoming, holder, axis=0)  45.1 us
    all_gather x1, blocking collectives, body(): table = lax.all_gather(pattern, 'rows', axis=1, tiled=True)  32.6 us
    all_to_all x5, starting transfers between devices, body(): lax.all_to_all(outgoing, 'rows', split_axis=0, concat_axis=0, tiled=True)  26.8 us
    dot_general x6, matrix products, solve_block(): jnp.einsum('psb,pbc->psc', rounded, inverse, preferred_element_type=jnp.f...  26.3 us
    psum x1, blocking collectives, body(): totals = lax.psum(local_sums, 'samp')  10.3 us
    all_to_all x5, waiting for transfers between devices, body(): lax.all_to_all(outgoing, 'rows', split_axis=0, concat_axis=0, tiled=True)  4.68 us
  transfers between devices with their start and end apart: 5, of which 2 were waited for; matrix products, arithmetic and copies ran while one was open for 41% of the time, Pallas kernels for 0%

commit v1 on v0

v1 whole, which is shorter than its diff:
```python
import functools

import jax
import jax.numpy as jnp
from jax import lax
from jax.experimental import pallas as pl
from jax.experimental.pallas import tpu as pltpu
from jax.sharding import PartitionSpec as P

MESH = pl.DeviceIdType.MESH
F32 = jnp.float32
BF16 = jnp.bfloat16


def farthest_first(n):
    return sorted(range(1, n), key=lambda o: -min(o, n - o))


def kernel(
    n, m, pat_ref, patv_ref, noise_hbm, diag_hbm, coup_hbm,
    samples_hbm, var_ref,
    noise, diag, coup, own, table, send, recv, need, want_v, want, sums, vrecv,
    noise_sem, diag_sem, coup_sem, out_sem, send_sem, recv_sem,
    nsend_sem, nrecv_sem, want_sem, vsend_sem, vrecv_sem,
):
    levels, slot_dev, samp, b = noise.shape
    fan = pat_ref.shape[2]
    me = lax.axis_index("rows")
    q = lax.axis_index("samp")
    order = farthest_first(n)

    def fetch(src, dst, sem, i):
        return pltpu.make_async_copy(src.at[i], dst.at[i], sem.at[i])

    for i in range(levels):
        fetch(noise_hbm, noise, noise_sem, i).start()
        fetch(diag_hbm, diag, diag_sem, i).start()
        if i > 0:
            fetch(coup_hbm, coup, coup_sem, i - 1).start()

    barrier = pltpu.get_barrier_semaphore()
    for o in range(1, n):
        pl.semaphore_signal(
            barrier, inc=1, device_id={"rows": lax.rem(me + o, n)}, device_id_type=MESH
        )
    for o in range(1, m):
        pl.semaphore_signal(
            barrier, inc=1, device_id={"samp": lax.rem(q + o, m)}, device_id_type=MESH
        )

    shape = (need.shape[0], need.shape[1], patv_ref.shape[1])
    dev = lax.broadcasted_iota(jnp.int32, shape, 0)
    lev = lax.broadcasted_iota(jnp.int32, shape, 1)
    key = lev * n + dev
    best = jnp.zeros(shape, jnp.int32)
    for t in range(levels - 1):
        entry = patv_ref[t : t + 1, :].reshape(1, 1, -1)
        holder = lax.div(entry, jnp.int32(slot_dev))
        slot = entry - holder * slot_dev
        best = jnp.maximum(best, jnp.where(holder == key, slot, 0))
    best = jnp.max(best, axis=2, keepdims=True)
    need[...] = jnp.broadcast_to(best, need.shape)
    want_v[0] = need[me]

    pl.semaphore_wait(barrier, n - 1 + m - 1)

    def need_copy(o):
        return pltpu.make_async_remote_copy(
            src_ref=need.at[lax.rem(me + o, n)],
            dst_ref=want_v.at[o],
            send_sem=nsend_sem.at[o],
            recv_sem=nrecv_sem.at[o],
            device_id={"rows": lax.rem(me + o, n)},
            device_id_type=MESH,
        )

    for o in order:
        need_copy(o).start()

    def block_copy(level, o):
        return pltpu.make_async_remote_copy(
            src_ref=send.at[level, o],
            dst_ref=recv.at[level, o],
            send_sem=send_sem.at[level, o],
            recv_sem=recv_sem.at[level, o],
            device_id={"rows": lax.rem(me + o, n)},
            device_id_type=MESH,
        )

    def finish(level, s, residual):
        x = jnp.dot(
            residual.astype(BF16), diag[level, s], preferred_element_type=F32
        ).astype(BF16)
        own[level, s] = x
        wide = x.astype(F32)
        sums[level, pl.ds(s, 1), :] = jnp.sum(wide * wide, axis=0, keepdims=True)

    def update(level, s):
        total = None
        for k in range(0, fan, 2):
            picked = [
                table[lax.div(pat_ref[level - 1, s, k + j], jnp.int32(slot_dev))]
                for j in range(2)
            ]
            part = jnp.dot(
                jnp.concatenate(picked, axis=1),
                coup[level - 1, s, pl.ds(k * b, 2 * b), :],
                preferred_element_type=F32,
            )
            total = part if total is None else total + part
        return total

    for level in range(levels):
        fetch(noise_hbm, noise, noise_sem, level).wait()
        fetch(diag_hbm, diag, diag_sem, level).wait()
        if level > 0:
            fetch(coup_hbm, coup, coup_sem, level - 1).wait()

        def row(s, carry, level=level):
            residual = noise[level, s].astype(F32)
            if level > 0:
                residual = residual - update(level, s)
            finish(level, s, residual)
            return carry

        lax.fori_loop(0, slot_dev, row, 0, unroll=2)

        if level == 0:
            for o in order:
                need_copy(o).wait()
            copy = pltpu.make_async_copy(want_v, want, want_sem)
            copy.start()
            copy.wait()

        if level < levels - 1:
            for o in order:
                send[level, o] = own[level, want[n - o, level, 0]]
                block_copy(level, o).start()
            table[level * n + me] = own[level, want[0, level, 0]]
        pltpu.make_async_copy(own.at[level], samples_hbm.at[level], out_sem.at[level]).start()
        if level < levels - 1:
            for o in reversed(order):
                block_copy(level, o).wait()
                table[level * n + lax.rem(me - o + n, n)] = recv[level, o]

    def var_copy(o):
        return pltpu.make_async_remote_copy(
            src_ref=sums,
            dst_ref=vrecv.at[o],
            send_sem=vsend_sem.at[o],
            recv_sem=vrecv_sem.at[o],
            device_id={"samp": lax.rem(q + o, m)},
            device_id_type=MESH,
        )

    for o in range(1, m):
        var_copy(o).start()
    vrecv[0] = sums[...]
    for o in range(1, m):
        var_copy(o).wait()
    total = vrecv[q]
    for j in range(1, m):
        total = total + vrecv[lax.rem(q - j + m, m)]
    var_ref[...] = total * (1.0 / (samp * m))
    for level in range(levels):
        pltpu.make_async_copy(own.at[level], samples_hbm.at[level], out_sem.at[level]).wait()


def body(n, m, noise, diag, coupling, pattern):
    levels, slot_dev, samp, b = noise.shape
    fan = coupling.shape[2]
    lead = -(-levels // 8) * 8
    any_spec = pl.BlockSpec(memory_space=pl.ANY)
    vmem_spec = pl.BlockSpec(memory_space=pltpu.VMEM)
    dma = pltpu.SemaphoreType.DMA
    coupling = coupling.reshape(levels - 1, slot_dev, fan * b, b)
    return pl.pallas_call(
        functools.partial(kernel, n, m),
        out_shape=(
            jax.ShapeDtypeStruct(noise.shape, BF16),
            jax.ShapeDtypeStruct((levels, slot_dev, b), F32),
        ),
        in_specs=[pl.BlockSpec(memory_space=pltpu.SMEM), vmem_spec, any_spec, any_spec, any_spec],
        out_specs=(any_spec, vmem_spec),
        scratch_shapes=[
            pltpu.VMEM(noise.shape, BF16),
            pltpu.VMEM(diag.shape, BF16),
            pltpu.VMEM(coupling.shape, BF16),
            pltpu.VMEM(noise.shape, BF16),
            pltpu.VMEM(((levels - 1) * n, samp, b), BF16),
            pltpu.VMEM((levels - 1, n, samp, b), BF16),
            pltpu.VMEM((levels - 1, n, samp, b), BF16),
            pltpu.VMEM((n, lead, 128), jnp.int32),
            pltpu.VMEM((n, lead, 128), jnp.int32),
            pltpu.SMEM((n, lead, 128), jnp.int32),
            pltpu.VMEM((levels, slot_dev, b), F32),
            pltpu.VMEM((m, levels, slot_dev, b), F32),
            dma((levels,)),
            dma((levels,)),
            dma((levels - 1,)),
            dma((levels,)),
            dma((levels - 1, n)),
            dma((levels - 1, n)),
            dma((n,)),
            dma((n,)),
            dma,
            dma((m,)),
            dma((m,)),
        ],
        compiler_params=pltpu.CompilerParams(
            collective_id=0, has_side_effects=True, vmem_limit_bytes=56 * 1024 * 1024
        ),
    )(pattern, pattern.reshape(levels - 1, slot_dev * fan), noise, diag, coupling)


def solution(mesh):
    placed = (
        P(None, "rows", "samp", None),
        P(None, "rows", None, None),
        P(None, "rows", None, None, None),
        P(None, "rows", None),
    )
    return jax.shard_map(
        functools.partial(body, mesh.shape["rows"], mesh.shape["samp"]),
        mesh=mesh,
        in_specs=placed,
        out_specs=(P(None, "rows", "samp", None), P(None, "rows", None)),
        check_vma=False,
    )
```

time: 214 us -> 67 us (0.31)
  matrix products: 80.1 us -> 0 us
  Pallas kernels: 0 us -> 61.3 us
  local copies, waits for them, and re-layouts: 49.7 us -> 4.74 us
  blocking collectives: 42.8 us -> 0 us
  starting transfers between devices: 26.8 us -> 0 us
  other arithmetic: 7.59 us -> 0 us
  waiting for transfers between devices: 4.68 us -> 0 us
    dot_general x16 -> x0, matrix products: 80.1 us -> none  [the longest x10 53.8 us: contribution(): jnp.einsum('pksb,pkbc->psc', picked, blocks, preferred_element_type=jnp.f...]
    pallas_call x0 -> x1, Pallas kernels: none -> 61.3 us  [body(): pl.pallas_call(functools.partial(kernel, n, m), out_shape=(jax.ShapeDtype...]
    gather x20 -> x0, local copies, waits for them, and re-layouts: 48.1 us -> none  [the longest x15 45.1 us: body(): picked = jnp.take(incoming, holder, axis=0)]
    all_gather x1 -> x0, blocking collectives: 32.6 us -> none  [body(): table = lax.all_gather(pattern, 'rows', axis=1, tiled=True)]
    all_to_all x5 -> x0, starting transfers between devices: 26.8 us -> none  [body(): lax.all_to_all(outgoing, 'rows', split_axis=0, concat_axis=0, tiled=True)]
    psum x1 -> x0, blocking collectives: 10.3 us -> none  [body(): totals = lax.psum(local_sums, 'samp')]
    all_to_all x5 -> x0, waiting for transfers between devices: 4.68 us -> none  [body(): lax.all_to_all(outgoing, 'rows', split_axis=0, concat_axis=0, tiled=True)]
    select_n x10 -> x0, other arithmetic: 3.99 us -> none  [body(): outgoing = jnp.take(block, wanted, axis=0)]
  transfers between devices with their start and end apart: 5 -> 0, of which waited for: 2 -> 0; matrix products, arithmetic and copies ran while one was open for 41% -> 0% of each run, Pallas kernels for 0% -> 0%
where the time goes in v1:
time: 67 us; the launch traced here: 66.7 us
  Pallas kernels  61.3 us (91%)
  local copies, waits for them, and re-layouts  4.74 us (7%)
    pallas_call x1, Pallas kernels, body(): pl.pallas_call(functools.partial(kernel, n, m), out_shape=(jax.ShapeDtype...  61.3 us
    unnamed x4, local copies, waits for them, and re-layouts  3.34 us
    reshape x1, local copies, waits for them, and re-layouts, body(): pattern.reshape(levels - 1, slot_dev * fan)  1.4 us

profile of v1, /device:TPU:0, one launch (start us, length us, event | category | flops | bytes accessed | tf_op | source)
XLA Modules:
  0.0 66.7 jit_solution(35236798334583192)
XLA Ops:
  0.6 1.4 %reshape.10.patv_ref = s32[5,128]{1,0:T(8,128)} reshape(s32[5,8,16]{2,1,0:T(8,128)} %pat_ref.1) | data formatting | bytes 5120 | tf_op jit(solution)/shard_map/reshape | solution.py:213
  2.0 61.3 %shard_map.59 = (bf16[6,8,128,128]{3,2,1,0:T(8,128)(2,1)}, f32[6,8,128]{2,1,0:T(8,128)}) custom-call(s32[5,8,16]{2,1,0:T(8,128)} %pat_ref.1, s32[5,128]{1,0:T(8,128)} %reshape.10.patv_ref, bf16[6,8,128,128]{3,2,1,0:T(8,128)(2,1)} %noise_hbm.1, bf16[6,8,128,128]{3,2,1,0:T(8,128)(2,1)} %diag_hbm.1, bf16[5,8,2048,128]{3,2,1,0:T(8,128)(2,1)} %bitcast.1), custom_call_target="tpu_custom_call" | custom-call | tf_op jit(solution)/shard_map/pallas_call | solution.py:177
  63.4 0.0 copy-start
  63.4 2.7 %copy.8 = bf16[6,8,128,128]{3,2,1,0:T(8,128)(2,1)} copy(bf16[6,8,128,128]{3,2,1,0:T(8,128)(2,1)} %get-tuple-element.4) | data formatting | bytes 3145728
  66.1 0.0 copy-done
  66.1 0.6 copy.9
Async XLA Ops:
  63.4 2.7 %copy-start = (f32[6,8,128]{2,1,0:T(8,128)S(1)}, f32[6,8,128]{2,1,0:T(8,128)}, u32[]{:S(2)}) copy-start(f32[6,8,128]{2,1,0:T(8,128)} %get-tuple-element.5) | copy-start | bytes 73732

commit v2 on v1

v2 whole, which is shorter than its diff:
```python
import functools

import jax
import jax.numpy as jnp
from jax import lax
from jax.experimental import pallas as pl
from jax.experimental.pallas import tpu as pltpu
from jax.sharding import PartitionSpec as P

MESH = pl.DeviceIdType.MESH
F32 = jnp.float32
BF16 = jnp.bfloat16


GROUP = 4


def kernel(
    n, m, pat_ref, patv_ref, noise_hbm, diag_hbm, coup_hbm,
    samples_hbm, var_ref,
    noise, diag, coup, own, table, send, recv, need, want_v, want, sums, vrecv,
    noise_sem, diag_sem, coup_sem, out_sem, send_sem, recv_sem,
    nsend_sem, nrecv_sem, want_sem, vsend_sem, vrecv_sem,
):
    levels, slot_dev, samp, b = noise.shape
    fan = pat_ref.shape[2]
    me = lax.axis_index("rows")
    q = lax.axis_index("samp")
    half = samp // 2

    def fetch(src, dst, sem, i):
        return pltpu.make_async_copy(src.at[i], dst.at[i], sem.at[i])

    for i in range(levels):
        fetch(noise_hbm, noise, noise_sem, i).start()
        fetch(diag_hbm, diag, diag_sem, i).start()
    for i in range(levels - 1):
        fetch(coup_hbm, coup, coup_sem, i).start()

    barrier = pltpu.get_barrier_semaphore()
    for o in range(1, n):
        pl.semaphore_signal(
            barrier, inc=1, device_id={"rows": lax.rem(me + o, n)}, device_id_type=MESH
        )
    for o in range(1, m):
        pl.semaphore_signal(
            barrier, inc=1, device_id={"samp": lax.rem(q + o, m)}, device_id_type=MESH
        )

    shape = (need.shape[0], need.shape[1], fan)
    dev = lax.broadcasted_iota(jnp.int32, shape, 0)
    lev = lax.broadcasted_iota(jnp.int32, shape, 1)
    key = lev * n + dev
    best = jnp.zeros(shape, jnp.int32)
    for t in range(levels - 1):
        for s in range(slot_dev):
            entry = patv_ref[t, s : s + 1, :].reshape(1, 1, fan)
            holder = lax.div(entry, jnp.int32(slot_dev))
            slot = entry - holder * slot_dev
            best = jnp.maximum(best, jnp.where(holder == key, slot, 0))
    best = jnp.max(best, axis=2, keepdims=True)
    need[...] = jnp.broadcast_to(best, need.shape)
    want_v[0] = need[me]

    def need_copy(o):
        return pltpu.make_async_remote_copy(
            src_ref=need.at[lax.rem(me + o, n)],
            dst_ref=want_v.at[o],
            send_sem=nsend_sem.at[o],
            recv_sem=nrecv_sem.at[o],
            device_id={"rows": lax.rem(me + o, n)},
            device_id_type=MESH,
        )

    def block_copy(level, h, o):
        return pltpu.make_async_remote_copy(
            src_ref=send.at[level, h, o],
            dst_ref=recv.at[level, h, o],
            send_sem=send_sem.at[level, h, o],
            recv_sem=recv_sem.at[level, h, o],
            device_id={"rows": lax.rem(me + o, n)},
            device_id_type=MESH,
        )

    def holder_of(level, s, k):
        return lax.div(pat_ref[level - 1, s, k], jnp.int32(slot_dev))

    def solve(level, s, halves):
        low, count = halves[0] * half, len(halves) * half
        residual = noise[level, s, pl.ds(low, count), :].astype(F32)
        if level > 0:
            total = None
            for k in range(0, fan, 2):
                picked = [
                    jnp.concatenate(
                        [table[h, holder_of(level, s, k + j)] for h in halves], axis=0
                    )
                    for j in range(2)
                ]
                part = jnp.dot(
                    jnp.concatenate(picked, axis=1),
                    coup[level - 1, s, pl.ds(k * b, 2 * b), :],
                    preferred_element_type=F32,
                )
                total = part if total is None else total + part
            residual = residual - total
        return jnp.dot(
            residual.astype(BF16), diag[level, s], preferred_element_type=F32
        ).astype(BF16)

    def own_rows(level, halves):
        low, count = halves[0] * half, len(halves) * half

        def row(s, carry):
            x = solve(level, s, halves)
            own[level, s, pl.ds(low, count), :] = x
            wide = x.astype(F32)
            part = jnp.sum(wide * wide, axis=0, keepdims=True)
            if low > 0:
                part = part + sums[level, pl.ds(s, 1), :]
            sums[level, pl.ds(s, 1), :] = part
            return carry

        lax.fori_loop(0, slot_dev, row, 0, unroll=8)

    def keep_own(level):
        mine = own[level, want[0, level, 0]]
        for h in range(2):
            table[h, level * n + me] = mine[h * half : (h + 1) * half]

    def receive(level, h):
        for o in range(1, n):
            block_copy(level, h, o).wait()
            table[h, level * n + lax.rem(me - o + n, n)] = recv[level, h, o]

    def write_out(level):
        return pltpu.make_async_copy(own.at[level], samples_hbm.at[level], out_sem.at[level])

    def loaded(level):
        fetch(noise_hbm, noise, noise_sem, level).wait()
        fetch(diag_hbm, diag, diag_sem, level).wait()
        if level > 0:
            fetch(coup_hbm, coup, coup_sem, level - 1).wait()

    loaded(0)
    own_rows(0, (0, 1))
    pl.semaphore_wait(barrier, n - 1 + m - 1)
    for o in range(1, n):
        need_copy(o).start()
    for o in range(1, n):
        need_copy(o).wait()
    copy = pltpu.make_async_copy(want_v, want, want_sem)
    copy.start()
    copy.wait()
    for h in range(2):
        for o in range(1, n):
            block = own[0, want[n - o, 0, 0]]
            send[0, h, o] = block[h * half : (h + 1) * half]
            block_copy(0, h, o).start()
    keep_own(0)
    write_out(0).start()

    for level in range(1, levels):
        loaded(level)
    for level in range(1, levels - 1):
        for h in range(2):
            receive(level - 1, h)
            for first in range(1, n, GROUP):
                group = range(first, min(first + GROUP, n))
                for o in group:
                    send[level, h, o] = solve(level, want[n - o, level, 0], (h,))
                for o in group:
                    block_copy(level, h, o).start()
        own_rows(level, (0, 1))
        keep_own(level)
        write_out(level).start()

    last = levels - 1
    for h in range(2):
        receive(last - 1, h)
        own_rows(last, (h,))
    write_out(last).start()

    def var_copy(o):
        return pltpu.make_async_remote_copy(
            src_ref=sums,
            dst_ref=vrecv.at[o],
            send_sem=vsend_sem.at[o],
            recv_sem=vrecv_sem.at[o],
            device_id={"samp": lax.rem(q + o, m)},
            device_id_type=MESH,
        )

    for o in range(1, m):
        var_copy(o).start()
    vrecv[0] = sums[...]
    for o in range(1, m):
        var_copy(o).wait()
    total = vrecv[q]
    for j in range(1, m):
        total = total + vrecv[lax.rem(q - j + m, m)]
    var_ref[...] = total * (1.0 / (samp * m))
    for level in range(levels):
        write_out(level).wait()


def body(n, m, noise, diag, coupling, pattern):
    levels, slot_dev, samp, b = noise.shape
    fan = coupling.shape[2]
    lead = -(-levels // 8) * 8
    any_spec = pl.BlockSpec(memory_space=pl.ANY)
    vmem_spec = pl.BlockSpec(memory_space=pltpu.VMEM)
    dma = pltpu.SemaphoreType.DMA
    coupling = coupling.reshape(levels - 1, slot_dev, fan * b, b)
    return pl.pallas_call(
        functools.partial(kernel, n, m),
        out_shape=(
            jax.ShapeDtypeStruct(noise.shape, BF16),
            jax.ShapeDtypeStruct((levels, slot_dev, b), F32),
        ),
        in_specs=[pl.BlockSpec(memory_space=pltpu.SMEM), vmem_spec, any_spec, any_spec, any_spec],
        out_specs=(any_spec, vmem_spec),
        scratch_shapes=[
            pltpu.VMEM(noise.shape, BF16),
            pltpu.VMEM(diag.shape, BF16),
            pltpu.VMEM(coupling.shape, BF16),
            pltpu.VMEM(noise.shape, BF16),
            pltpu.VMEM((2, (levels - 1) * n, samp // 2, b), BF16),
            pltpu.VMEM((levels - 1, 2, n, samp // 2, b), BF16),
            pltpu.VMEM((levels - 1, 2, n, samp // 2, b), BF16),
            pltpu.VMEM((n, lead, 128), jnp.int32),
            pltpu.VMEM((n, lead, 128), jnp.int32),
            pltpu.SMEM((n, lead, 128), jnp.int32),
            pltpu.VMEM((levels, slot_dev, b), F32),
            pltpu.VMEM((m, levels, slot_dev, b), F32),
            dma((levels,)),
            dma((levels,)),
            dma((levels - 1,)),
            dma((levels,)),
            dma((levels - 1, 2, n)),
            dma((levels - 1, 2, n)),
            dma((n,)),
            dma((n,)),
            dma,
            dma((m,)),
            dma((m,)),
        ],
        compiler_params=pltpu.CompilerParams(
            collective_id=0, has_side_effects=True, vmem_limit_bytes=56 * 1024 * 1024
        ),
    )(pattern, pattern, noise, diag, coupling)


def solution(mesh):
    placed = (
        P(None, "rows", "samp", None),
        P(None, "rows", None, None),
        P(None, "rows", None, None, None),
        P(None, "rows", None),
    )
    return jax.shard_map(
        functools.partial(body, mesh.shape["rows"], mesh.shape["samp"]),
        mesh=mesh,
        in_specs=placed,
        out_specs=(P(None, "rows", "samp", None), P(None, "rows", None)),
        check_vma=False,
    )
```

time: 67 us -> 56.7 us (0.85)
  Pallas kernels: 61.3 us -> 52.4 us
  local copies, waits for them, and re-layouts: 4.74 us -> 3.34 us
    pallas_call x1, Pallas kernels: 61.3 us -> 52.4 us  [body(): pl.pallas_call(functools.partial(kernel, n, m), out_shape=(jax.ShapeDtype...]
    reshape x1 -> x0, local copies, waits for them, and re-layouts: 1.4 us -> none  [body(): pattern.reshape(levels - 1, slot_dev * fan)]
where the time goes in v2:
time: 56.7 us; the launch traced here: 56.4 us
  Pallas kernels  52.4 us (92%)
  local copies, waits for them, and re-layouts  3.34 us (6%)
  between operations  0.65 us (1%)
    pallas_call x1, Pallas kernels, body(): pl.pallas_call(functools.partial(kernel, n, m), out_shape=(jax.ShapeDtype...  52.4 us
    unnamed x4, local copies, waits for them, and re-layouts  3.34 us

profile of v2, /device:TPU:0, one launch (start us, length us, event | category | flops | bytes accessed | tf_op | source)
XLA Modules:
  0.0 56.4 jit_solution(6863856235360314880)
XLA Ops:
  0.6 52.4 %shard_map.59 = (bf16[6,8,128,128]{3,2,1,0:T(8,128)(2,1)}, f32[6,8,128]{2,1,0:T(8,128)}) custom-call(s32[5,8,16]{2,1,0:T(8,128)} %patv_ref.1, s32[5,8,16]{2,1,0:T(8,128)} %patv_ref.1, bf16[6,8,128,128]{3,2,1,0:T(8,128)(2,1)} %noise_hbm.1, bf16[6,8,128,128]{3,2,1,0:T(8,128)(2,1)} %diag_hbm.1, bf16[5,8,2048,128]{3,2,1,0:T(8,128)(2,1)} %bitcast.1), custom_call_target="tpu_custom_call" | custom-call | tf_op jit(solution)/shard_map/pallas_call | solution.py:215
  53.1 0.0 copy-start
  53.1 2.7 %copy.8 = bf16[6,8,128,128]{3,2,1,0:T(8,128)(2,1)} copy(bf16[6,8,128,128]{3,2,1,0:T(8,128)(2,1)} %get-tuple-element.4) | data formatting | bytes 3145728
  55.8 0.0 copy-done
  55.8 0.6 %copy.9 = f32[6,8,128]{2,1,0:T(8,128)} copy(f32[6,8,128]{2,1,0:T(8,128)S(1)} %copy-done) | data formatting | bytes 49152
Async XLA Ops:
  53.1 2.7 %copy-start = (f32[6,8,128]{2,1,0:T(8,128)S(1)}, f32[6,8,128]{2,1,0:T(8,128)}, u32[]{:S(2)}) copy-start(f32[6,8,128]{2,1,0:T(8,128)} %get-tuple-element.5) | copy-start | bytes 73732

commit v3 on v2

--- a/solution.py
+++ b/solution.py
@@ -204,6 +204,25 @@
         write_out(level).wait()
 
 
+def hand_out(x_hbm, v_hbm, y_hbm, w_hbm, x, v, in_sem, out_sem, v_sem):
+    levels = x.shape[0]
+    reads = [pltpu.make_async_copy(x_hbm.at[i], x.at[i], in_sem.at[i]) for i in range(levels)]
+    writes = [pltpu.make_async_copy(x.at[i], y_hbm.at[i], out_sem.at[i]) for i in range(levels)]
+    v_read = pltpu.make_async_copy(v_hbm, v, v_sem.at[0])
+    v_write = pltpu.make_async_copy(v, w_hbm, v_sem.at[1])
+    v_read.start()
+    for copy in reads:
+        copy.start()
+    v_read.wait()
+    v_write.start()
+    for i in range(levels):
+        reads[i].wait()
+        writes[i].start()
+    v_write.wait()
+    for copy in writes:
+        copy.wait()
+
+
 def body(n, m, noise, diag, coupling, pattern):
     levels, slot_dev, samp, b = noise.shape
     fan = coupling.shape[2]
@@ -212,7 +231,7 @@
     vmem_spec = pl.BlockSpec(memory_space=pltpu.VMEM)
     dma = pltpu.SemaphoreType.DMA
     coupling = coupling.reshape(levels - 1, slot_dev, fan * b, b)
-    return pl.pallas_call(
+    solved = pl.pallas_call(
         functools.partial(kernel, n, m),
         out_shape=(
             jax.ShapeDtypeStruct(noise.shape, BF16),
@@ -249,6 +268,19 @@
             collective_id=0, has_side_effects=True, vmem_limit_bytes=56 * 1024 * 1024
         ),
     )(pattern, pattern, noise, diag, coupling)
+    return pl.pallas_call(
+        hand_out,
+        out_shape=tuple(jax.ShapeDtypeStruct(a.shape, a.dtype) for a in solved),
+        in_specs=[any_spec, any_spec],
+        out_specs=(any_spec, any_spec),
+        scratch_shapes=[
+            pltpu.VMEM(solved[0].shape, BF16),
+            pltpu.VMEM(solved[1].shape, F32),
+            dma((levels,)),
+            dma((levels,)),
+            dma((2,)),
+        ],
+    )(*solved)
 
 
 def solution(mesh):

time: 56.7 us -> 55.9 us (0.986)
  local copies, waits for them, and re-layouts: 3.34 us -> 0 us
  Pallas kernels: 52.4 us -> 54.9 us
    unnamed x4 -> x0, local copies, waits for them, and re-layouts: 3.34 us -> none
    pallas_call x0 -> x1, Pallas kernels: none -> 2.44 us  [body(): pl.pallas_call(hand_out, out_shape=tuple((jax.ShapeDtypeStruct(a.shape, a...]
where the time goes in v3:
time: 55.9 us; the launch traced here: 55.7 us
  Pallas kernels  54.9 us (98%)
  between operations  0.8 us (1%)
    pallas_call x1, Pallas kernels, body(): pl.pallas_call(functools.partial(kernel, n, m), out_shape=(jax.ShapeDtype...  52.5 us
    pallas_call x1, Pallas kernels, body(): pl.pallas_call(hand_out, out_shape=tuple((jax.ShapeDtypeStruct(a.shape, a...  2.44 us

profile of v3, /device:TPU:0, one launch (start us, length us, event | category | flops | bytes accessed | tf_op | source)
XLA Modules:
  0.0 55.7 jit_solution(6703797244123408834)
XLA Ops:
  0.6 52.5 %shard_map.59 = (bf16[6,8,128,128]{3,2,1,0:T(8,128)(2,1)}, f32[6,8,128]{2,1,0:T(8,128)}) custom-call(s32[5,8,16]{2,1,0:T(8,128)} %patv_ref.1, s32[5,8,16]{2,1,0:T(8,128)} %patv_ref.1, bf16[6,8,128,128]{3,2,1,0:T(8,128)(2,1)} %noise_hbm.1, bf16[6,8,128,128]{3,2,1,0:T(8,128)(2,1)} %diag_hbm.1, bf16[5,8,2048,128]{3,2,1,0:T(8,128)(2,1)} %bitcast.1), custom_call_target="tpu_custom_call" | custom-call | tf_op jit(solution)/shard_map/pallas_call | solution.py:234
  53.1 2.4 %shard_map.60 = (bf16[6,8,128,128]{3,2,1,0:T(8,128)(2,1)}, f32[6,8,128]{2,1,0:T(8,128)}) custom-call(bf16[6,8,128,128]{3,2,1,0:T(8,128)(2,1)} %get-tuple-element.4.x_hbm, f32[6,8,128]{2,1,0:T(8,128)} %get-tuple-element.5.v_hbm), custom_call_target="tpu_custom_call" | custom-call | tf_op jit(solution)/shard_map/pallas_call | solution.py:271
